TPU v7x, 32 devices: a whole 2x2x4 slice. The times are simulated.
32 devices in a mesh: parts: 2 (over x), seq: 8 (over z, y), head: 2 (over core).
Axes of the slice: x: 2, y: 2, z: 4, core: 2. Of those that a mesh axis runs over, the one named last changes fastest.
Arguments:
- latents: bfloat16 [8192, 2112], P(('parts', 'seq', 'head')), parts along dimension 0, may hold values from -400 to 400
- q_gain: float32 [1536], replicated, may hold values from 0.25 to 1.75
- kv_gain: float32 [512], replicated, may hold values from 0.25 to 1.75
- q_weight: bfloat16 [2, 1536, 32, 192], P('head', None, 'seq'), may hold values from -0.15625 to 0.15625
- kv_weight: bfloat16 [2, 512, 32, 256], P('head', None, 'seq'), may hold values from -0.25 to 0.25
- lengths: int32 [16, 8], P('parts'), parts along dimension 0, may hold values from 0 to 512, as said below
Outputs:
- attended: bfloat16 [8192, 8192], P(('parts', 'seq'), 'head'), parts along dimension 0
There are 2 independent parts, one for each index of `parts`. A program takes and returns all parts, laid end to end along the dimension named above; an argument that names none is the same for every part. Nothing has to cross between parts.
Inputs may be any that keep to these rules, and one draw needn't show every extreme that they name: Row g lists the lengths of the sequences packed in order in group g: they sum to 512, each is a multiple of 64, the nonzero ones come first. Some group holds a single sequence of 512 tokens; the group after it holds two sequences of 256 tokens, and the group 8 / 2 after that one holds 8 sequences of 64 tokens.
All inputs are finite; a program needn't handle non-finite values.
Results may differ from a plain program's by a relative error of at most 0.011.
Values may be sent and summed in bfloat16 or wider, within the bound.
A program may use at most 128 MiB of HBM per device.

v0:
```python
from functools import partial
import math

import jax
import jax.numpy as jnp
from jax import lax
from jax.sharding import PartitionSpec as P

epsilon = 1e-06


def rotary(values, positions):
    half_width = values.shape[-1] // 2
    freq_table = jnp.exp(
        jnp.arange(half_width, dtype=jnp.float32) * (-2.0 * jnp.log(10000.0) / values.shape[-1])
    )
    angles = positions.astype(jnp.float32)[:, None] * freq_table[None, :]
    if values.ndim == 3:
        angles = angles[:, None, :]
    cosine = jnp.cos(angles)
    sine_part = jnp.sin(angles)
    first_half = values[..., :half_width]
    second_half = values[..., half_width:]
    return jnp.concatenate(
        [
            first_half * cosine - second_half * sine_part,
            second_half * cosine + first_half * sine_part,
        ],
        axis=-1,
    )


def normalize(part_values, gain_vec):
    squares = jnp.mean(part_values * part_values, axis=-1, keepdims=True)
    return (part_values * lax.rsqrt(squares + epsilon) * gain_vec).astype(jnp.bfloat16)


def seq_starts(length_row, token_count):
    seq_ends = jnp.cumsum(length_row)
    begins = seq_ends - length_row
    token_ids = jnp.arange(token_count, dtype=jnp.int32)
    inside = (token_ids[:, None] >= begins[None, :]) & (token_ids[:, None] < seq_ends[None, :])
    return jnp.sum(jnp.where(inside, begins[None, :], 0), axis=1)


def prepare(block_rows, q_gain, kv_gain, positions):
    q_width = q_gain.shape[0]
    kv_width = kv_gain.shape[0]
    q_part = block_rows[:, :q_width].astype(jnp.float32)
    kv_part = block_rows[:, q_width : q_width + kv_width].astype(jnp.float32)
    rope_part = block_rows[:, q_width + kv_width :].astype(jnp.float32)
    return (
        normalize(q_part, q_gain),
        normalize(kv_part, kv_gain),
        rotary(rope_part, positions).astype(jnp.bfloat16),
    )


def rotate_tail(projected, positions, rope_width):
    nope_width = projected.shape[2] - rope_width
    return jnp.concatenate(
        [projected[:, :, :nope_width], rotary(projected[:, :, nope_width:], positions)], axis=-1
    )


def tile_scores(
    query_nope, query_rope, key_nope, rope_keys, begins, score_scale, row_span, col_span
):
    row_low, row_high = row_span
    col_low, col_high = col_span
    part_scores = jnp.einsum(
        "qhd,khd->hqk", query_nope, key_nope, preferred_element_type=jnp.float32
    )
    part_scores = part_scores + jnp.einsum(
        "qhd,kd->hqk", query_rope, rope_keys, preferred_element_type=jnp.float32
    )
    row_ids = jnp.arange(row_low, row_high, dtype=jnp.int32)
    col_ids = jnp.arange(col_low, col_high, dtype=jnp.int32)
    allowed = (begins[row_low:row_high, None] <= col_ids[None, :]) & (
        col_ids[None, :] <= row_ids[:, None]
    )
    return jnp.where(allowed[None], part_scores * score_scale, -jnp.inf)


def softmax_parts(scores):
    maxima = jnp.max(scores, axis=-1, keepdims=True)
    exp_terms = jnp.exp(scores - maxima)
    return (exp_terms.astype(jnp.bfloat16), jnp.sum(exp_terms, axis=-1))


def head_block(queries, key_values, rope_keys, begins):
    token_count = queries.shape[0]
    rope_width = rope_keys.shape[1]
    nope_width = queries.shape[2] - rope_width
    score_scale = queries.shape[2] ** (-0.5)
    value_part = key_values[:, :, nope_width:]
    scorer = partial(
        tile_scores,
        queries[:, :, :nope_width],
        queries[:, :, nope_width:],
        key_values[:, :, :nope_width],
        rope_keys,
        begins,
        score_scale,
    )
    softmax_num, totals = softmax_parts(scorer((0, token_count), (0, token_count)))
    mixed_out = jnp.einsum(
        "hqk,khd->qhd", softmax_num, value_part, preferred_element_type=jnp.float32
    )
    return (mixed_out / totals.T[:, :, None]).astype(jnp.bfloat16)


def heads_attention(queries, key_values, rope_keys, begins):
    token_count = queries.shape[0]
    head_count = queries.shape[1]
    block_heads = math.gcd(4, head_count)
    value_width = key_values.shape[2] - (queries.shape[2] - rope_keys.shape[1])

    def block_step(block_index, collected):
        mixed_out = head_block(queries, key_values, rope_keys, begins)
        return mixed_out

    collected = lax.fori_loop(
        0,
        head_count // block_heads,
        block_step,
        jnp.zeros((token_count, head_count, value_width), jnp.bfloat16),
    )
    return collected.reshape(token_count, head_count * value_width)


def shards(latents, q_gain, kv_gain, q_weight, kv_weight, lengths):
    rope_width = latents.shape[1] - q_gain.shape[0] - kv_gain.shape[0]
    group_count = lengths.shape[0]
    token_count = latents.shape[0] * lax.axis_size("head")
    total_tokens = token_count * group_count
    local_heads = q_weight.shape[2]
    begins_all = jax.vmap(partial(seq_starts, token_count=token_count))(lengths)
    positions_all = (jnp.arange(token_count, dtype=jnp.int32)[None, :] - begins_all).reshape(
        total_tokens
    )
    q_normed, kv_normed, rope_keys = prepare(
        lax.all_gather(latents, ("seq", "head"), axis=0, tiled=True), q_gain, kv_gain, positions_all
    )
    projected = jnp.einsum("tc,chd->thd", q_normed, q_weight[0], preferred_element_type=jnp.float32)
    queries = rotate_tail(projected, positions_all, rope_width).astype(jnp.bfloat16)
    key_values = jnp.einsum(
        "tc,chd->thd", kv_normed, kv_weight[0], preferred_element_type=jnp.float32
    ).astype(jnp.bfloat16)
    value_width = kv_weight.shape[3] - (q_weight.shape[3] - rope_width)

    def group_step(group_index, collected):
        row_low = group_index * token_count
        query_rows = lax.dynamic_slice_in_dim(queries, row_low, token_count, 0)
        pair_rows = lax.dynamic_slice_in_dim(key_values, row_low, token_count, 0)
        rope_rows = lax.dynamic_slice_in_dim(rope_keys, row_low, token_count, 0)
        begin_row = lax.dynamic_index_in_dim(begins_all, group_index, 0, keepdims=False)
        mixed_out = heads_attention(query_rows, pair_rows, rope_rows, begin_row)
        return lax.dynamic_update_slice_in_dim(collected, mixed_out, row_low, 0)

    mixed_all = lax.fori_loop(
        0,
        group_count,
        group_step,
        jnp.zeros((total_tokens, local_heads * value_width), jnp.bfloat16),
    )
    return lax.all_to_all(mixed_all, "seq", split_axis=0, concat_axis=1, tiled=True)


def solution(mesh):
    return jax.shard_map(
        shards,
        mesh=mesh,
        in_specs=(
            P(("parts", "seq", "head"), None),
            P(),
            P(),
            P("head", None, "seq", None),
            P("head", None, "seq", None),
            P("parts", None),
        ),
        out_specs=P(("parts", "seq"), "head"),
        check_vma=False,
    )
```

profile of v0, /device:TPU:0, one launch (start us, length us, event | category | flops | bytes accessed | tf_op | source)
XLA Modules:
  0.0 366.6 jit_solution(16817115893242284728)
XLA Ops:
  6.5 0.7 all-gather.2.cloned.1.call-update
  7.3 0.8 reduce_window_sum.11
  8.1 0.7 sub.47
  9.0 100.7 %all-gather.2.cloned.1.call-done = bf16[4096,2112]{0,1:T(8,128)(2,1)} async-done(((bf16[256,2112]{0,1:T(8,128)(2,1)}), bf16[4096,2112]{0,1:T(8,128)(2,1)}) %all-gather.2.cloned.1.call-update) | async-done | bytes 17301520 | tf_op jit(solution)/shard_map/all_gather | solution.py:143
  109.7 7.2 %fusion.27 = f32[4096]{0:T(1024)S(1)} fusion(bf16[4096,2112]{0,1:T(8,128)(2,1)} %all-gather.2.cloned.1.call-done), kind=kLoop, calls=%fused_computation.28 | loop fusion | flops 18870272 | bytes 12599296 | tf_op jit(solution)/shard_map/reduce_sum | solution.py:34
  117.0 16.1 %fusion.30 = f32[4096,768]{0,1} fusion(bf16[1536,768]{0,1:T(8,128)(2,1)S(1)} %bitcast.46, f32[1536]{0:T(1024)S(1)} %copy-done.3, f32[4096]{0:T(1024)S(1)} %add_rsqrt_fusion, bf16[4096,2112]{0,1:T(8,128)(2,1)} %all-gather.2.cloned.1.call-done), kind=kOutput, calls=%fused_computation.31 | convolution fusion | flops 9688842240 | bytes 27547648
  133.0 6.0 %slice.96 = bf16[4096,4,128]{0,2,1:T(8,128)(2,1)} slice(f32[4096,4,192]{0,2,1:T(8,128)} %bitcast.52), slice={[0:4096], [0:4], [0:128]} | slice | bytes 8388608 | tf_op jit(solution)/shard_map/slice | solution.py:62
  139.1 0.9 fusion.35
  140.1 2.1 subtract_convert_fusion.1
  142.2 2.9 subtract_convert_fusion
  145.2 0.4 copy-done.2
  145.7 5.5 %pad_maximum_fusion = bf16[4096,4,192]{0,2,1:T(8,128)(2,1)} fusion(bf16[4096,4,32]{0,2,1:T(8,128)(2,1)S(1)} %get-tuple-element.181, bf16[4096,4,32]{0,2,1:T(8,128)(2,1)S(1)} %get-tuple-element.180, bf16[4096,4,128]{0,2,1:T(8,128)(2,1)S(1)} %copy-done.2), kind=kLoop, calls=%fused_computation.42 | loop fusion | flops 18874368 | bytes 12582912 | tf_op jit(solution)/shard_map/concatenate | solution.py:61
  151.2 8.2 %convolution_convert_fusion = bf16[4096,4,256]{2,0,1:T(8,128)(2,1)} fusion(f32[512]{0:T(512)S(1)} %copy-done.4, f32[4096]{0:T(1024)S(1)} %add_rsqrt_fusion.1, bf16[4096,2112]{0,1:T(8,128)(2,1)S(1)} %bitcast.48, bf16[512,4,256]{2,1,0:T(4,128)(2,1)} %bitcast.57), kind=kOutput, calls=%fused_computation.41 | convolution fusion | flops 4307550208 | bytes 13649920 | tf_op jit(solution)/shard_map/tc,chd->thd/dot_general | solution.py:147
  159.4 2.3 broadcast_in_dim.83.clone
  161.7 86.8 %while.21 = (s32[]{:T(128)}, bf16[4096,512]{1,0:T(8,128)(2,1)}, bf16[4096,4,256]{2,0,1:T(8,128)(2,1)}, s32[8,512]{1,0:T(8,128)S(1)}, bf16[4096,4,192]{0,2,1:T(8,...) while((s32[]{:T(128)}, bf16[4096,512]{1,0:T(8,128)(2,1)}, ...), condition=%wide.region_7.8_spmd, body=%wide.region_4.7_spmd.sunk | while | flops 680783872 | bytes 26067640 | solution.py:161
  161.7 3.9 %fusion.60 = f32[4,512,512]{1,2,0:T(8,128)} fusion(bf16[4096,4,192]{0,2,1:T(8,128)(2,1)} %get-tuple-element.253, s32[]{:T(128)S(6)} %select_n.33, bf16[4096,4,256]{2,0,1:T(8,128)(2,1)} %get-tuple-element.251), kind=kOutput, calls=%fused_computation.14.clone.1 | convolution fusion | flops 268435456 | bytes 5243904 | tf_op jit(solution)/shard_map/while/body/eval_jaxpr/while/body/eval_jaxpr/qhd,khd->hqk/dot_general | solution.py:71
  165.7 3.4 fusion.62
  169.0 0.6 fusion.63
  169.6 1.8 fusion.64
  171.5 0.2 copy.58
  171.7 0.8 constant_dynamic-update-slice_fusion.2
  172.5 3.9 %fusion.60 = f32[4,512,512]{1,2,0:T(8,128)} fusion(bf16[4096,4,192]{0,2,1:T(8,128)(2,1)} %get-tuple-element.253, s32[]{:T(128)S(6)} %select_n.33, bf16[4096,4,256]{2,0,1:T(8,128)(2,1)} %get-tuple-element.251), kind=kOutput, calls=%fused_computation.14.clone.1 | convolution fusion | flops 268435456 | bytes 5243904 | tf_op jit(solution)/shard_map/while/body/eval_jaxpr/while/body/eval_jaxpr/qhd,khd->hqk/dot_general | solution.py:71
  176.5 3.4 fusion.62
  179.9 0.6 fusion.63
  180.5 1.8 fusion.64
  182.3 0.2 copy.58
  182.5 0.8 constant_dynamic-update-slice_fusion.2
  183.4 3.8 %fusion.60 = f32[4,512,512]{1,2,0:T(8,128)} fusion(bf16[4096,4,192]{0,2,1:T(8,128)(2,1)} %get-tuple-element.253, s32[]{:T(128)S(6)} %select_n.33, bf16[4096,4,256]{2,0,1:T(8,128)(2,1)} %get-tuple-element.251), kind=kOutput, calls=%fused_computation.14.clone.1 | convolution fusion | flops 268435456 | bytes 5243904 | tf_op jit(solution)/shard_map/while/body/eval_jaxpr/while/body/eval_jaxpr/qhd,khd->hqk/dot_general | solution.py:71
  187.4 3.4 fusion.62
  190.7 0.6 fusion.63
  191.3 1.8 fusion.64
  193.2 0.2 copy.58
  193.4 0.8 constant_dynamic-update-slice_fusion.2
  194.2 3.8 %fusion.60 = f32[4,512,512]{1,2,0:T(8,128)} fusion(bf16[4096,4,192]{0,2,1:T(8,128)(2,1)} %get-tuple-element.253, s32[]{:T(128)S(6)} %select_n.33, bf16[4096,4,256]{2,0,1:T(8,128)(2,1)} %get-tuple-element.251), kind=kOutput, calls=%fused_computation.14.clone.1 | convolution fusion | flops 268435456 | bytes 5243904 | tf_op jit(solution)/shard_map/while/body/eval_jaxpr/while/body/eval_jaxpr/qhd,khd->hqk/dot_general | solution.py:71
  198.2 3.4 fusion.62
  201.6 0.6 fusion.63
  202.2 1.8 fusion.64
  204.0 0.2 copy.58
  204.2 0.8 constant_dynamic-update-slice_fusion.2
  205.0 3.8 %fusion.60 = f32[4,512,512]{1,2,0:T(8,128)} fusion(bf16[4096,4,192]{0,2,1:T(8,128)(2,1)} %get-tuple-element.253, s32[]{:T(128)S(6)} %select_n.33, bf16[4096,4,256]{2,0,1:T(8,128)(2,1)} %get-tuple-element.251), kind=kOutput, calls=%fused_computation.14.clone.1 | convolution fusion | flops 268435456 | bytes 5243904 | tf_op jit(solution)/shard_map/while/body/eval_jaxpr/while/body/eval_jaxpr/qhd,khd->hqk/dot_general | solution.py:71
  209.0 3.4 fusion.62
  212.4 0.6 fusion.63
  213.0 1.8 fusion.64
  214.8 0.2 copy.58
  215.1 0.8 constant_dynamic-update-slice_fusion.2
  215.9 3.8 %fusion.60 = f32[4,512,512]{1,2,0:T(8,128)} fusion(bf16[4096,4,192]{0,2,1:T(8,128)(2,1)} %get-tuple-element.253, s32[]{:T(128)S(6)} %select_n.33, bf16[4096,4,256]{2,0,1:T(8,128)(2,1)} %get-tuple-element.251), kind=kOutput, calls=%fused_computation.14.clone.1 | convolution fusion | flops 268435456 | bytes 5243904 | tf_op jit(solution)/shard_map/while/body/eval_jaxpr/while/body/eval_jaxpr/qhd,khd->hqk/dot_general | solution.py:71
  219.9 3.4 fusion.62
  223.3 0.6 fusion.63
  223.8 1.8 fusion.64
  225.9 0.8 constant_dynamic-update-slice_fusion.2
  226.7 3.8 %fusion.60 = f32[4,512,512]{1,2,0:T(8,128)} fusion(bf16[4096,4,192]{0,2,1:T(8,128)(2,1)} %get-tuple-element.253, s32[]{:T(128)S(6)} %select_n.33, bf16[4096,4,256]{2,0,1:T(8,128)(2,1)} %get-tuple-element.251), kind=kOutput, calls=%fused_computation.14.clone.1 | convolution fusion | flops 268435456 | bytes 5243904 | tf_op jit(solution)/shard_map/while/body/eval_jaxpr/while/body/eval_jaxpr/qhd,khd->hqk/dot_general | solution.py:71
  230.7 3.4 fusion.62
  234.1 0.6 fusion.63
  234.7 1.8 fusion.64
  236.8 0.8 constant_dynamic-update-slice_fusion.2
  237.6 3.8 %fusion.60 = f32[4,512,512]{1,2,0:T(8,128)} fusion(bf16[4096,4,192]{0,2,1:T(8,128)(2,1)} %get-tuple-element.253, s32[]{:T(128)S(6)} %select_n.33, bf16[4096,4,256]{2,0,1:T(8,128)(2,1)} %get-tuple-element.251), kind=kOutput, calls=%fused_computation.14.clone.1 | convolution fusion | flops 268435456 | bytes 5243904 | tf_op jit(solution)/shard_map/while/body/eval_jaxpr/while/body/eval_jaxpr/qhd,khd->hqk/dot_general | solution.py:71
  241.6 3.4 fusion.62
  245.0 0.6 fusion.63
  245.5 1.8 fusion.64
  247.4 0.2 copy.58
  247.6 0.8 constant_dynamic-update-slice_fusion.2
  248.4 98.3 %all_to_all.19 = bf16[8,512,512]{2,1,0:T(8,128)(2,1)} all-to-all(bf16[8,512,512]{2,1,0:T(8,128)(2,1)} %bitcast.49), channel_id=1, replica_groups=mesh['parts'=2,'seq'=8,'head'=2] {'seq'}, dimensions={0} | all-to-all | bytes 8388608 | tf_op jit(solution)/shard_map/all_to_all | solution.py:167
  346.7 6.5 %copy.41 = bf16[8,512,512]{1,2,0:T(8,128)(2,1)} copy(bf16[8,512,512]{2,1,0:T(8,128)(2,1)} %all_to_all.19) | data formatting | bytes 8388608 | tf_op jit(solution)/shard_map/all_to_all | solution.py:167
  353.2 6.5 %copy.42 = bf16[512,4096]{1,0:T(8,128)(2,1)} copy(bf16[512,4096]{0,1:T(8,128)(2,1)} %bitcast.50) | data formatting | bytes 8388608 | tf_op jit(solution)/shard_map/all_to_all | solution.py:167
  (47 shorter events, 1.9 us)
Async XLA Ops:
  6.5 110.4 %copy-start = (bf16[1,1536,4,192]{1,3,2,0:T(8,128)(2,1)S(1)}, bf16[1,1536,4,192]{1,3,2,0:T(8,128)(2,1)}, u32[]{:S(2)}) copy-start(bf16[1,1536,4,192]{1,3,2,0:T(8,128)(2,1)} %param.11) | copy-start | bytes 7077892
  6.5 103.2 %all-gather.2.cloned.1.call-start = ((), (), s32[]{:S(2)}) async-start(), calls=%async_computation.1 | async-start | bytes 18382848 | tf_op jit(solution)/shard_map/all_gather | solution.py:143
  9.0 107.9 %copy-start.3 = (f32[1536]{0:T(1024)S(1)}, f32[1536]{0:T(1024)}, u32[]{:S(2)}) copy-start(f32[1536]{0:T(1024)} %param.9) | copy-start | bytes 18436
  109.7 29.4 %slice-start = ((s8[17301504]{0:T(1024)(128)(4,1)}), s8[524288]{0:T(1024)(128)(4,1)S(1)}, s32[]{:S(2)}) async-start(s8[17301504]{0:T(1024)(128)(4,1)} %bitcast.47), calls=%async_computation.2 | async-start | bytes 1048576
  116.9 22.1 %slice-start.1 = ((s8[17301504]{0:T(1024)(128)(4,1)}), s8[4194304]{0:T(1024)(128)(4,1)S(1)}, s32[]{:S(2)}) async-start(s8[17301504]{0:T(1024)(128)(4,1)} %bitcast.47), calls=%async_computation.3 | async-start | bytes 8388608
  116.9 22.1 %slice-start.2 = ((s8[17301504]{0:T(1024)(128)(4,1)}), s8[4194304]{0:T(1024)(128)(4,1)S(1)}, s32[]{:S(2)}) async-start(s8[17301504]{0:T(1024)(128)(4,1)} %bitcast.47), calls=%async_computation.4 | async-start | bytes 8388608
  116.9 22.1 %slice-start.3 = ((s8[17301504]{0:T(1024)(128)(4,1)}), s8[4194304]{0:T(1024)(128)(4,1)S(1)}, s32[]{:S(2)}) async-start(s8[17301504]{0:T(1024)(128)(4,1)} %bitcast.47), calls=%async_computation.5 | async-start | bytes 8388608
  116.9 22.1 %slice-start.4 = ((s8[17301504]{0:T(1024)(128)(4,1)}), s8[4194304]{0:T(1024)(128)(4,1)S(1)}, s32[]{:S(2)}) async-start(s8[17301504]{0:T(1024)(128)(4,1)} %bitcast.47), calls=%async_computation.6 | async-start | bytes 8388608
  142.2 3.5 copy-start.2
  145.7 5.5 %copy-start.4 = (f32[512]{0:T(512)S(1)}, f32[512]{0:T(512)}, u32[]{:S(2)}) copy-start(f32[512]{0:T(512)} %param.10) | copy-start | bytes 6148
  353.2 6.5 %copy-start.1 = (bf16[1,1536,4,192]{1,3,2,0:T(8,128)(2,1)S(1)}, bf16[1,1536,4,192]{1,3,2,0:T(8,128)(2,1)}, u32[]{:S(2)}) copy-start(bf16[1,1536,4,192]{1,3,2,0:T(8,128)(2,1)} %param.11) | copy-start | bytes 7077892
Sparse Core Ops, SparseCore 0:
  8.8 100.8 all-gather.1
where the time goes:
time: 368 us; the launch traced here: 367 us
  waiting for transfers between devices  101 us (27%)
  blocking collectives  98.3 us (27%)
  matrix products  96.7 us (26%)
  local copies, waits for them, and re-layouts  30.2 us (8%)
  other arithmetic  26.1 us (7%)
  between operations  13.6 us (4%)
    all_gather x1, waiting for transfers between devices, shards(): lax.all_gather(latents, ('seq', 'head'), axis=0, tiled=True)  101 us
    all_to_all x1, blocking collectives, shards(): lax.all_to_all(mixed_all, 'seq', split_axis=0, concat_axis=1, tiled=True)  98.3 us
    dot_general x8, matrix products, tile_scores(): jnp.einsum('qhd,khd->hqk', query_nope, key_nope, preferred_element_type=j...  30.8 us
    dot_general x8, matrix products, tile_scores(): jnp.einsum('qhd,kd->hqk', query_rope, rope_keys, preferred_element_type=j...  27 us
    unnamed x1, matrix products  16.1 us
    dot_general x8, matrix products, head_block(): jnp.einsum('hqk,khd->qhd', softmax_num, value_part, preferred_element_typ...  14.7 us
    all_to_all x2, local copies, waits for them, and re-layouts, shards(): lax.all_to_all(mixed_all, 'seq', split_axis=0, concat_axis=1, tiled=True)  13 us
    dynamic_update_slice x16, local copies, waits for them, and re-layouts, group_step(): return lax.dynamic_update_slice_in_dim(collected, mixed_out, row_low, 0)  8.37 us
  transfers between devices with their start and end apart: 1, of which 1 were waited for; matrix products, arithmetic and copies ran while one was open for 0% of the time, Pallas kernels for 0%

commit v1 on v0

v1 whole, which is shorter than its diff:
```python
import functools
import math

import jax
import jax.numpy as jnp
import numpy as np
from jax import lax
from jax.experimental import pallas as pl
from jax.experimental.pallas import tpu as pltpu
from jax.sharding import PartitionSpec as P

EPSILON = 1e-06
MASKED = -1e30
CHUNKS = 3
MESH = pl.DeviceIdType.MESH


def kernel(
    n_line, nh, q_width, kv_width, rope, nope, vd, tokens, slots,
    lengths, freqs, q_gain, kv_gain, latents, wq, wkv,
    out,
    wq_buf, wkv_buf, lat, qn, kvn, cosine, sine, kr, bias, q_s, k_s, v_s, obuf,
    own_sem, lat_send, lat_recv, line_send, line_recv, x_send, x_recv, out_local, out_send, out_recv,
):
    part = lax.axis_index("parts")
    seq = lax.axis_index("seq")
    core = lax.axis_index("head")
    half = lax.rem(part, 2)
    pos = seq // 2
    parity = lax.rem(seq, 2)
    pair = {"seq": seq + 1 - 2 * parity}
    sibling = {"head": 1 - core}
    across = {"parts": part + 1 - 2 * half}
    left = {"seq": jnp.maximum(seq - 2, parity)}
    right = {"seq": jnp.minimum(seq + 2, 2 * (n_line - 1) + parity)}
    has_left = pos > 0
    has_right = pos < n_line - 1
    half_tokens = tokens // 2
    q_rows = q_width // 4
    kv_rows = kv_width // 2

    def piece(q_ref, kv_ref, side, chunk):
        if chunk < 2:
            start = pl.multiple_of(side * (2 * q_rows) + chunk * q_rows, q_rows)
            return q_ref.at[pl.ds(start, q_rows), :]
        return kv_ref.at[pl.ds(pl.multiple_of(side * kv_rows, kv_rows), kv_rows), :]

    def slot(block, side, chunk):
        return piece(wq_buf.at[block], wkv_buf.at[block], side, chunk)

    def line_copy(block, chunk, direction):
        return pltpu.make_async_remote_copy(
            src_ref=slot(block, half, chunk), dst_ref=slot(block, half, chunk),
            send_sem=line_send.at[direction, block, chunk], recv_sem=line_recv.at[block, chunk],
            device_id=(left, right)[direction], device_id_type=MESH,
        )

    def own_line_copy(chunk, direction):
        return pltpu.make_async_remote_copy(
            src_ref=piece(wq, wkv, half, chunk), dst_ref=slot(pos, half, chunk),
            send_sem=line_send.at[direction, pos, chunk], recv_sem=line_recv.at[pos, chunk],
            device_id=(left, right)[direction], device_id_type=MESH,
        )

    def x_copy(block, chunk, side):
        return pltpu.make_async_remote_copy(
            src_ref=slot(block, side, chunk), dst_ref=slot(block, side, chunk),
            send_sem=x_send.at[block, chunk], recv_sem=x_recv.at[block, chunk],
            device_id=across, device_id_type=MESH,
        )

    def lat_copy(source, group, owner, target, index):
        return pltpu.make_async_remote_copy(
            src_ref=source, dst_ref=lat.at[group, owner],
            send_sem=lat_send.at[index], recv_sem=lat_recv.at[index],
            device_id=target, device_id_type=MESH,
        )

    barrier = pltpu.get_barrier_semaphore()
    for target in (pair, sibling, across):
        pl.semaphore_signal(barrier, inc=1, device_id=target, device_id_type=MESH)

    @pl.when(has_left)
    def _():
        pl.semaphore_signal(barrier, inc=1, device_id=left, device_id_type=MESH)

    @pl.when(has_right)
    def _():
        pl.semaphore_signal(barrier, inc=1, device_id=right, device_id_type=MESH)

    own_lat = pltpu.make_async_copy(latents, lat.at[0, core], own_sem.at[0])
    own_wq = pltpu.make_async_copy(wq, wq_buf.at[pos], own_sem.at[1])
    own_wkv = pltpu.make_async_copy(wkv, wkv_buf.at[pos], own_sem.at[2])
    own_lat.start()
    own_wq.start()
    own_wkv.start()

    pl.semaphore_wait(barrier, 3 + has_left.astype(jnp.int32) + has_right.astype(jnp.int32))

    lat_copy(latents, 0, core, sibling, 0).start()
    lat_copy(latents, 1, core, pair, 1).start()

    @pl.when(has_left)
    def _():
        for chunk in range(CHUNKS):
            own_line_copy(chunk, 0).start()

    @pl.when(has_right)
    def _():
        for chunk in range(CHUNKS):
            own_line_copy(chunk, 1).start()

    def forward(distance, chunk):
        @pl.when(pos - distance >= 0)
        def _():
            block = jnp.maximum(pos - distance, 0)
            line_copy(block, chunk, 1).wait_recv()

            @pl.when(has_right)
            def _():
                line_copy(block, chunk, 1).start()

            x_copy(block, chunk, half).start()

        @pl.when(pos + distance < n_line)
        def _():
            block = jnp.minimum(pos + distance, n_line - 1)
            line_copy(block, chunk, 0).wait_recv()

            @pl.when(has_left)
            def _():
                line_copy(block, chunk, 0).start()

            x_copy(block, chunk, half).start()

    unit = tokens // slots

    def tables(group):
        index = jnp.where(group == 0, seq, seq + 1 - 2 * parity)
        spans = []
        begin = jnp.int32(0)
        for i in range(slots):
            end = begin + lengths[index, i]
            spans.append((begin, end))
            begin = end

        def begins_of(ids):
            found = jnp.zeros_like(ids)
            for low, high in spans:
                found = jnp.where((ids >= low) & (ids < high), low, found)
            return found

        freq = freqs[...]
        fine = lax.broadcasted_iota(jnp.int32, (unit, 128), 0).astype(jnp.float32) * freq
        fine_cos, fine_sin = jnp.cos(fine), jnp.sin(fine)
        coarse_ids = lax.broadcasted_iota(jnp.int32, (slots, 128), 0) * unit
        coarse = (coarse_ids - begins_of(coarse_ids)).astype(jnp.float32) * freq
        coarse_cos, coarse_sin = jnp.cos(coarse), jnp.sin(coarse)
        lanes = lax.broadcasted_iota(jnp.int32, (unit, 128), 1)
        sign = jnp.where(lanes < 64, -1.0, 1.0).astype(jnp.float32)
        for i in range(slots):
            c, s = coarse_cos[i : i + 1], coarse_sin[i : i + 1]
            cosine[group, pl.ds(i * unit, unit), :] = fine_cos * c - fine_sin * s
            sine[group, pl.ds(i * unit, unit), :] = (fine_sin * c + fine_cos * s) * sign
        for i in range(slots):
            rows = lax.broadcasted_iota(jnp.int32, (unit, tokens), 0) + i * unit
            cols = lax.broadcasted_iota(jnp.int32, (unit, tokens), 1)
            first = begins_of(jnp.full((1, tokens), i * unit, jnp.int32))
            allowed = (first <= cols) & (cols <= rows)
            bias[group, pl.ds(i * unit, unit), :] = jnp.where(allowed, 0.0, MASKED).astype(jnp.float32)

    def normalize(group, owner):
        step_rows = 64

        def step(i, carry):
            source = pl.ds(pl.multiple_of(i * step_rows, step_rows), step_rows)
            target = pl.ds(pl.multiple_of(owner * half_tokens + i * step_rows, step_rows), step_rows)
            q_part = lat[group, owner, source, 0:q_width].astype(jnp.float32)
            squares = jnp.mean(q_part * q_part, axis=-1, keepdims=True)
            qn[group, target, :] = (q_part * lax.rsqrt(squares + EPSILON) * q_gain[...]).astype(jnp.bfloat16)
            kv_part = lat[group, owner, source, q_width : q_width + kv_width].astype(jnp.float32)
            squares = jnp.mean(kv_part * kv_part, axis=-1, keepdims=True)
            kvn[group, target, :] = (kv_part * lax.rsqrt(squares + EPSILON) * kv_gain[...]).astype(jnp.bfloat16)
            tail = lat[group, owner, source, q_width + kv_width :].astype(jnp.float32)
            turned = tail * cosine[group, target, :] + pltpu.roll(tail, 64, 1) * sine[group, target, :]
            lanes = lax.broadcasted_iota(jnp.int32, turned.shape, 1)
            first = lax.rem(lanes, 64) < 32
            kr[group, 0, target, :] = jnp.where(first, turned, 0.0).astype(jnp.bfloat16)
            kr[group, 1, target, :] = jnp.where(first, 0.0, turned).astype(jnp.bfloat16)
            return carry

        lax.fori_loop(0, half_tokens // step_rows, step, 0)

    factor = (nope + rope) ** (-0.5) * math.log2(math.e)
    tile = tokens // 2

    def attend(block, group):
        for j in range(nh // 2):
            for r in range(2):
                rows = pl.ds(r * tile, tile)
                q = jnp.dot(
                    qn[group, rows, :], wq_buf[block, :, j * 384 : (j + 1) * 384],
                    preferred_element_type=jnp.float32,
                )
                tail = q[:, 2 * nope :]
                turned = tail * cosine[group, rows, :] + pltpu.roll(tail, 64, 1) * sine[group, rows, :]
                turned = turned.astype(jnp.bfloat16)
                for a in range(2):
                    q_s[a, rows, 0:nope] = q[:, a * nope : (a + 1) * nope].astype(jnp.bfloat16)
                    q_s[a, rows, nope:] = turned
                width = nope + vd
                kv = jnp.dot(
                    kvn[group, rows, :], wkv_buf[block, :, j * 2 * width : (j + 1) * 2 * width],
                    preferred_element_type=jnp.float32,
                ).astype(jnp.bfloat16)
                for a in range(2):
                    k_s[a, rows, 0:nope] = kv[:, a * width : a * width + nope]
                    k_s[a, rows, nope:] = kr[group, a, rows, :]
                    v_s[a, rows, :] = kv[:, a * width + nope : (a + 1) * width]
            for a in range(2):
                for r in range(2):
                    rows = pl.ds(r * tile, tile)
                    span = (r + 1) * tile
                    scores = lax.dot_general(
                        q_s[a, rows, :], k_s[a, 0:span, :], (((1,), (1,)), ((), ())),
                        preferred_element_type=jnp.float32,
                    )
                    scores = scores + bias[group, rows, 0:span]
                    top = jnp.max(scores, axis=-1, keepdims=True)
                    terms = jnp.exp2((scores - top) * factor)
                    total = jnp.sum(terms, axis=-1, keepdims=True)
                    mixed = jnp.dot(
                        terms.astype(jnp.bfloat16), v_s[a, 0:span, :], preferred_element_type=jnp.float32
                    )
                    at = (2 * j + a) * vd
                    obuf[group, block, rows, at : at + vd] = (mixed / total).astype(jnp.bfloat16)

    def columns(block):
        width = nh * vd
        return pl.ds(pl.multiple_of((2 * block + parity) * width, width), width)

    def local_out(block):
        return pltpu.make_async_copy(obuf.at[0, block], out.at[:, columns(block)], out_local.at[block])

    def pair_out(block):
        return pltpu.make_async_remote_copy(
            src_ref=obuf.at[1, block], dst_ref=out.at[:, columns(block)],
            send_sem=out_send.at[block], recv_sem=out_recv.at[block],
            device_id=pair, device_id_type=MESH,
        )

    def pair_out_wait(block):
        width = nh * vd
        span = pl.ds(pl.multiple_of((2 * block + 1 - parity) * width, width), width)
        return pltpu.make_async_remote_copy(
            src_ref=obuf.at[1, block], dst_ref=out.at[:, span],
            send_sem=out_send.at[block], recv_sem=out_recv.at[block],
            device_id=pair, device_id_type=MESH,
        )

    lax.fori_loop(0, 2, lambda g, c: (tables(g), c)[1], 0)
    own_lat.wait()
    normalize(0, core)
    lat_copy(latents, 0, 1 - core, sibling, 0).wait_recv()
    normalize(0, 1 - core)
    own_wq.wait()
    own_wkv.wait()

    def own_step(g, carry):
        @pl.when(g == 1)
        def _():
            forward(1, 0)
            lat_copy(latents, 1, core, pair, 1).wait_recv()
            lat_copy(lat.at[1, core], 1, core, sibling, 2).start()
            normalize(1, core)
            lat_copy(lat.at[1, 1 - core], 1, 1 - core, sibling, 2).wait_recv()
            normalize(1, 1 - core)
            forward(1, 1)

        attend(pos, g)
        return carry

    lax.fori_loop(0, 2, own_step, 0)
    local_out(pos).start()
    pair_out(pos).start()
    forward(1, 2)

    def stage(t, carry):
        @pl.when(t < n_line)
        def _():
            for chunk in range(CHUNKS):
                forward(t, chunk)

        def side(s, inner):
            block = pos + (2 * s - 1) * (t - 1)

            @pl.when((block >= 0) & (block < n_line))
            def _():
                held = jnp.clip(block, 0, n_line - 1)
                for chunk in range(CHUNKS):
                    x_copy(held, chunk, 1 - half).wait_recv()

                def group_step(i, rest):
                    attend(held, 1 - i)

                    @pl.when(i == 0)
                    def _():
                        pair_out(held).start()

                    return rest

                lax.fori_loop(0, 2, group_step, 0)
                local_out(held).start()

            return inner

        return lax.fori_loop(0, 2, side, carry)

    lax.fori_loop(2, n_line + 1, stage, 0)

    lat_copy(latents, 0, core, sibling, 0).wait_send()
    lat_copy(latents, 1, core, pair, 1).wait_send()
    lat_copy(lat.at[1, core], 1, core, sibling, 2).wait_send()

    def drain(block, carry):
        @pl.when((block <= pos) & has_right)
        def _():
            for chunk in range(CHUNKS):
                line_copy(block, chunk, 1).wait_send()

        @pl.when((block >= pos) & has_left)
        def _():
            for chunk in range(CHUNKS):
                line_copy(block, chunk, 0).wait_send()

        @pl.when(block != pos)
        def _():
            for chunk in range(CHUNKS):
                x_copy(block, chunk, half).wait_send()

        local_out(block).wait()
        pair_out(block).wait_send()
        pair_out_wait(block).wait_recv()
        return carry

    lax.fori_loop(0, n_line, drain, 0)


def shards(latents, q_gain, kv_gain, q_weight, kv_weight, lengths):
    q_width, kv_width = q_gain.shape[0], kv_gain.shape[0]
    rope = latents.shape[1] - q_width - kv_width
    nh = q_weight.shape[2]
    nope = q_weight.shape[3] - rope
    vd = kv_weight.shape[3] - nope
    n_seq = lax.axis_size("seq")
    n_line = n_seq // 2
    half_tokens = latents.shape[0]
    tokens = half_tokens * lax.axis_size("head")
    slots = lengths.shape[1]
    r = rope // 2

    body = q_width + kv_width
    first, second = latents[:, body : body + r], latents[:, body + r :]
    lat = jnp.concatenate([latents[:, :body], first, first, second, second], axis=1)
    wide = lat.shape[1]
    q4 = q_weight[0].reshape(q_width, nh // 2, 2, nope + rope)
    wq = jnp.concatenate(
        [
            q4[:, :, 0, :nope], q4[:, :, 1, :nope],
            q4[:, :, 0, nope : nope + r], q4[:, :, 1, nope : nope + r],
            q4[:, :, 0, nope + r :], q4[:, :, 1, nope + r :],
        ],
        axis=-1,
    ).reshape(q_width, nh * (nope + rope))
    wkv = kv_weight[0].reshape(kv_width, nh * (nope + vd))
    base = 10000.0 ** (-2.0 * np.arange(r) / rope)
    freqs = jnp.asarray(np.tile(base, 4)[None, :], jnp.float32)

    vmem = pl.BlockSpec(memory_space=pltpu.VMEM)
    hbm = pl.BlockSpec(memory_space=pl.ANY)
    bf16, f32, dma = jnp.bfloat16, jnp.float32, pltpu.SemaphoreType.DMA
    heads_total = nh * n_seq
    return pl.pallas_call(
        functools.partial(kernel, n_line, nh, q_width, kv_width, rope, nope, vd, tokens, slots),
        out_shape=jax.ShapeDtypeStruct((tokens, heads_total * vd), bf16),
        in_specs=[pl.BlockSpec(memory_space=pltpu.SMEM), vmem, vmem, vmem, hbm, hbm, hbm],
        out_specs=hbm,
        scratch_shapes=[
            pltpu.VMEM((n_line,) + wq.shape, bf16),
            pltpu.VMEM((n_line,) + wkv.shape, bf16),
            pltpu.VMEM((2, 2, half_tokens, wide), bf16),
            pltpu.VMEM((2, tokens, q_width), bf16),
            pltpu.VMEM((2, tokens, kv_width), bf16),
            pltpu.VMEM((2, tokens, 128), f32),
            pltpu.VMEM((2, tokens, 128), f32),
            pltpu.VMEM((2, 2, tokens, 128), bf16),
            pltpu.VMEM((2, tokens, tokens), f32),
            pltpu.VMEM((2, tokens, nope + 128), bf16),
            pltpu.VMEM((2, tokens, nope + 128), bf16),
            pltpu.VMEM((2, tokens, vd), bf16),
            pltpu.VMEM((2, n_line, tokens, nh * vd), bf16),
            dma((3,)), dma((3,)), dma((3,)),
            dma((2, n_line, CHUNKS)), dma((n_line, CHUNKS)),
            dma((n_line, CHUNKS)), dma((n_line, CHUNKS)),
            dma((n_line,)), dma((n_line,)), dma((n_line,)),
        ],
        compiler_params=pltpu.CompilerParams(
            collective_id=0, has_side_effects=True, vmem_limit_bytes=60 * 1024 * 1024
        ),
    )(lengths, freqs, q_gain[None, :], kv_gain[None, :], lat, wq, wkv)


def solution(mesh):
    return jax.shard_map(
        shards,
        mesh=mesh,
        in_specs=(
            P(("parts", "seq", "head"), None),
            P(),
            P(),
            P("head", None, "seq", None),
            P("head", None, "seq", None),
            P("parts", None),
        ),
        out_specs=P(("parts", "seq"), "head"),
        check_vma=False,
    )
```

time: 368 us -> 194 us (0.53)
  Pallas kernels: 0 us -> 150 us
  waiting for transfers between devices: 101 us -> 0 us
  blocking collectives: 98.3 us -> 0 us
  matrix products: 96.7 us -> 0 us
  other arithmetic: 26.1 us -> 0 us
  between operations: 13.6 us -> 0.09 us
  local copies, waits for them, and re-layouts: 30.2 us -> 42.2 us
    pallas_call x0 -> x1, Pallas kernels: none -> 150 us  [shards(): pl.pallas_call(functools.partial(kernel, n_line, nh, q_width, kv_width, r...]
    all_gather x1 -> x0, waiting for transfers between devices: 101 us -> none  [shards(): lax.all_gather(latents, ('seq', 'head'), axis=0, tiled=True)]
    all_to_all x1 -> x0, blocking collectives: 98.3 us -> none  [shards(): lax.all_to_all(mixed_all, 'seq', split_axis=0, concat_axis=1, tiled=True)]
    dot_general x25 -> x0, matrix products: 80.7 us -> none  [the longest x8 30.8 us: tile_scores(): jnp.einsum('qhd,khd->hqk', query_nope, key_nope, preferred_element_type=j...]
    concatenate x0 -> x2, local copies, waits for them, and re-layouts: none -> 20.5 us  [the longest x1 18.6 us: shards(): jnp.concatenate([q4[:, :, 0, :nope], q4[:, :, 1, :nope], q4[:, :, 0, nope...]
    unnamed x21 -> x16, local copies, waits for them, and re-layouts: 0.49 us -> 18.3 us
    unnamed x1 -> x0, matrix products: 16.1 us -> none
    all_to_all x2 -> x0, local copies, waits for them, and re-layouts: 13 us -> none  [shards(): lax.all_to_all(mixed_all, 'seq', split_axis=0, concat_axis=1, tiled=True)]
  transfers between devices with their start and end apart: 1 -> 0, of which waited for: 1 -> 0; matrix products, arithmetic and copies ran while one was open for 0% -> 0% of each run, Pallas kernels for 0% -> 0%
where the time goes in v1:
time: 194 us; the launch traced here: 192 us
  Pallas kernels  150 us (77%)
  local copies, waits for them, and re-layouts  42.2 us (22%)
    pallas_call x1, Pallas kernels, shards(): pl.pallas_call(functools.partial(kernel, n_line, nh, q_width, kv_width, r...  150 us
    concatenate x1, local copies, waits for them, and re-layouts, shards(): jnp.concatenate([q4[:, :, 0, :nope], q4[:, :, 1, :nope], q4[:, :, 0, nope...  18.6 us
    unnamed x16, local copies, waits for them, and re-layouts  18.3 us

profile of v1, /device:TPU:0, one launch (start us, length us, event | category | flops | bytes accessed | tf_op | source)
XLA Modules:
  0.0 192.4 jit_solution(17977181745114165802)
XLA Ops:
  0.0 1.3 fusion
  1.3 1.8 copy.22
  3.1 1.7 copy.23
  4.8 1.7 copy.24
  6.5 1.8 copy.25
  8.3 1.5 fusion.1
  9.8 0.6 copy.20
  10.4 1.8 copy.21
  12.2 18.6 %concatenate.7 = bf16[1536,2,384]{2,1,0:T(2,128)(2,1)S(1)} concatenate(bf16[1536,2,128]{2,1,0:T(2,128)(2,1)S(1)} %bitcast.16, bf16[1536,2,128]{2,1,0:T(2,128)(2,1)} %bitcast.17, bf16[1536,2,32]{2,1,0:T(2,128)(2,1)} %bitcast.18, bf16[1536,2,32]{2,1,0:T(2,128)(2,1)} %bitcast.19, bf16[1536,2,32]{2,1,0:T(2,128)(2,1)} %bitcast.20, bf16[1536,2,32]{2,1,0:T(2,128)(2,1)} %bitcast.21), dimensions={2} | concatenate | bytes 4718592 | tf_op jit(solution)/shard_map/concatenate | solution.py:367
  30.8 0.0 slice-start
  30.8 1.9 copy.26
  32.7 0.0 slice-start.1
  32.7 0.0 slice-start.2
  32.7 0.0 slice-done
  32.7 0.0 copy-start
  32.7 0.8 copy.17
  33.5 0.0 copy-start.1
  33.5 0.0 slice-done.1
  33.6 0.1 copy.18
  33.7 0.0 slice-done.2
  33.7 0.1 copy.19
  33.8 1.9 concatenate.6.latents
  35.7 0.0 copy-done
  35.7 1.2 copy.27
  36.9 0.0 copy-done.1
  37.0 0.6 broadcast_in_dim.6.q_gain
  37.5 150.2 %shard_map.73 = bf16[512,4096]{1,0:T(8,128)(2,1)} custom-call(s32[8,8]{1,0:T(8,128)} %lengths.1, f32[1,128]{1,0:T(1,128)} %constant.2.clone.freqs, f32[1,1536]{1,0:T(1,128)} %broadcast_in_dim.6.q_gain, f32[1,512]{1,0:T(1,128)} %bitcast.25, bf16[256,2176]{1,0:T(8,128)(2,1)} %concatenate.6.latents, bf16[1536,768]{1,0:T(8,128)(2,1)} %bitcast.13, ...), custom_call_target="tpu_custom_call" | custom-call | tf_op jit(solution)/shard_map/pallas_call | solution.py:383
  187.7 4.7 %copy.29 = bf16[512,4096]{1,0:T(8,128)(2,1)} copy(bf16[512,4096]{1,0:T(8,128)(2,1)} %shard_map.73) | data formatting | bytes 8388608
Async XLA Ops:
  30.8 1.9 slice-start
  32.7 0.8 slice-start.1
  32.7 1.0 slice-start.2
  32.7 3.0 %copy-start = (bf16[1,512,4,256]{3,2,1,0:T(4,128)(2,1)S(1)}, bf16[1,512,4,256]{3,2,1,0:T(4,128)(2,1)}, u32[]{:S(2)}) copy-start(bf16[1,512,4,256]{3,2,1,0:T(4,128)(2,1)} %param.11) | copy-start | bytes 3145732
  33.5 3.4 %copy-start.1 = (f32[1536]{0:T(1024)S(1)}, f32[1536]{0:T(1024)}, u32[]{:S(2)}) copy-start(f32[1536]{0:T(1024)} %param.8) | copy-start | bytes 18436

commit v2 on v1

--- a/solution.py
+++ b/solution.py
@@ -11,7 +11,7 @@
 
 EPSILON = 1e-06
 MASKED = -1e30
-CHUNKS = 3
+CHUNKS = 6
 MESH = pl.DeviceIdType.MESH
 
 
@@ -36,17 +36,19 @@
     has_left = pos > 0
     has_right = pos < n_line - 1
     half_tokens = tokens // 2
-    q_rows = q_width // 4
+    per = nh // 2
+    split = per % 2 == 0
+    head = nope + rope
+    width = nope + vd
+    r = rope // 2
+    q_rows = nh * head // 8
     kv_rows = kv_width // 2
 
-    def piece(q_ref, kv_ref, side, chunk):
-        if chunk < 2:
-            start = pl.multiple_of(side * (2 * q_rows) + chunk * q_rows, q_rows)
-            return q_ref.at[pl.ds(start, q_rows), :]
-        return kv_ref.at[pl.ds(pl.multiple_of(side * kv_rows, kv_rows), kv_rows), :]
-
     def slot(block, side, chunk):
-        return piece(wq_buf.at[block], wkv_buf.at[block], side, chunk)
+        if chunk < 4:
+            start = pl.multiple_of(side * (4 * q_rows) + chunk * q_rows, q_rows)
+            return wq_buf.at[block, pl.ds(start, q_rows), :]
+        return wkv_buf.at[block, side, pl.ds((chunk - 4) * kv_rows, kv_rows), :]
 
     def line_copy(block, chunk, direction):
         return pltpu.make_async_remote_copy(
@@ -55,13 +57,6 @@
             device_id=(left, right)[direction], device_id_type=MESH,
         )
 
-    def own_line_copy(chunk, direction):
-        return pltpu.make_async_remote_copy(
-            src_ref=piece(wq, wkv, half, chunk), dst_ref=slot(pos, half, chunk),
-            send_sem=line_send.at[direction, pos, chunk], recv_sem=line_recv.at[pos, chunk],
-            device_id=(left, right)[direction], device_id_type=MESH,
-        )
-
     def x_copy(block, chunk, side):
         return pltpu.make_async_remote_copy(
             src_ref=slot(block, side, chunk), dst_ref=slot(block, side, chunk),
@@ -89,26 +84,36 @@
         pl.semaphore_signal(barrier, inc=1, device_id=right, device_id_type=MESH)
 
     own_lat = pltpu.make_async_copy(latents, lat.at[0, core], own_sem.at[0])
-    own_wq = pltpu.make_async_copy(wq, wq_buf.at[pos], own_sem.at[1])
-    own_wkv = pltpu.make_async_copy(wkv, wkv_buf.at[pos], own_sem.at[2])
+    own = []
+    for h in range(nh):
+        j, a = h // 2, h % 2
+        for start, size, at in (
+            (0, nope, a * nope), (nope, r, 2 * nope + a * r), (nope + r, r, 2 * nope + 2 * r + a * r)
+        ):
+            own.append((wq.at[pl.ds(h * head + start, size), :], wq_buf.at[pos, pl.ds(2 * j * head + at, size), :]))
+    for side in range(2):
+        own.append((wkv.at[:, pl.ds(side * per * width, per * width)], wkv_buf.at[pos, side]))
+    own = [pltpu.make_async_copy(*ends, own_sem.at[1 + i]) for i, ends in enumerate(own)]
     own_lat.start()
-    own_wq.start()
-    own_wkv.start()
+    for copy in own:
+        copy.start()
 
     pl.semaphore_wait(barrier, 3 + has_left.astype(jnp.int32) + has_right.astype(jnp.int32))
 
     lat_copy(latents, 0, core, sibling, 0).start()
     lat_copy(latents, 1, core, pair, 1).start()
+    for copy in own:
+        copy.wait()
 
     @pl.when(has_left)
     def _():
         for chunk in range(CHUNKS):
-            own_line_copy(chunk, 0).start()
+            line_copy(pos, chunk, 0).start()
 
     @pl.when(has_right)
     def _():
         for chunk in range(CHUNKS):
-            own_line_copy(chunk, 1).start()
+            line_copy(pos, chunk, 1).start()
 
     def forward(distance, chunk):
         @pl.when(pos - distance >= 0)
@@ -182,8 +187,10 @@
             squares = jnp.mean(kv_part * kv_part, axis=-1, keepdims=True)
             kvn[group, target, :] = (kv_part * lax.rsqrt(squares + EPSILON) * kv_gain[...]).astype(jnp.bfloat16)
             tail = lat[group, owner, source, q_width + kv_width :].astype(jnp.float32)
+            tail = jnp.concatenate([tail, tail], axis=1)
+            lanes = lax.broadcasted_iota(jnp.int32, tail.shape, 1)
+            tail = jnp.where((lanes >= r) & (lanes < 3 * r), pltpu.roll(tail, r, 1), tail)
             turned = tail * cosine[group, target, :] + pltpu.roll(tail, 64, 1) * sine[group, target, :]
-            lanes = lax.broadcasted_iota(jnp.int32, turned.shape, 1)
             first = lax.rem(lanes, 64) < 32
             kr[group, 0, target, :] = jnp.where(first, turned, 0.0).astype(jnp.bfloat16)
             kr[group, 1, target, :] = jnp.where(first, 0.0, turned).astype(jnp.bfloat16)
@@ -194,67 +201,65 @@
     factor = (nope + rope) ** (-0.5) * math.log2(math.e)
     tile = tokens // 2
 
-    def attend(block, group):
-        for j in range(nh // 2):
-            for r in range(2):
-                rows = pl.ds(r * tile, tile)
-                q = jnp.dot(
-                    qn[group, rows, :], wq_buf[block, :, j * 384 : (j + 1) * 384],
+    def attend(block, group, j):
+        q_at = pl.ds(pl.multiple_of(j * 2 * head, 2 * head), 2 * head)
+        for i in range(2):
+            rows = pl.ds(i * tile, tile)
+            q = lax.dot_general(
+                qn[group, rows, :], wq_buf[block, q_at, :], (((1,), (1,)), ((), ())),
+                preferred_element_type=jnp.float32,
+            )
+            tail = q[:, 2 * nope :]
+            turned = tail * cosine[group, rows, :] + pltpu.roll(tail, 64, 1) * sine[group, rows, :]
+            turned = turned.astype(jnp.bfloat16)
+            for a in range(2):
+                q_s[a, rows, 0:nope] = q[:, a * nope : (a + 1) * nope].astype(jnp.bfloat16)
+                q_s[a, rows, nope:] = turned
+                if split:
+                    side, at = j // (per // 2), lax.rem(j, per // 2) * 2 + a
+                else:
+                    side, at = (2 * j + a) // per, lax.rem(2 * j + a, per)
+                if per <= 2:
+                    at = a if split else 0
+                    kv_at = pl.ds(at * width, width)
+                else:
+                    kv_at = pl.ds(pl.multiple_of(at * width, width), width)
+                kv = jnp.dot(
+                    kvn[group, rows, :], wkv_buf[block, side, :, kv_at],
+                    preferred_element_type=jnp.float32,
+                ).astype(jnp.bfloat16)
+                k_s[a, rows, 0:nope] = kv[:, 0:nope]
+                k_s[a, rows, nope:] = kr[group, a, rows, :]
+                v_s[a, rows, :] = kv[:, nope:]
+        for a in range(2):
+            for i in range(2):
+                rows = pl.ds(i * tile, tile)
+                span = (i + 1) * tile
+                scores = lax.dot_general(
+                    q_s[a, rows, :], k_s[a, 0:span, :], (((1,), (1,)), ((), ())),
                     preferred_element_type=jnp.float32,
                 )
-                tail = q[:, 2 * nope :]
-                turned = tail * cosine[group, rows, :] + pltpu.roll(tail, 64, 1) * sine[group, rows, :]
-                turned = turned.astype(jnp.bfloat16)
-                for a in range(2):
-                    q_s[a, rows, 0:nope] = q[:, a * nope : (a + 1) * nope].astype(jnp.bfloat16)
-                    q_s[a, rows, nope:] = turned
-                width = nope + vd
-                kv = jnp.dot(
-                    kvn[group, rows, :], wkv_buf[block, :, j * 2 * width : (j + 1) * 2 * width],
-                    preferred_element_type=jnp.float32,
-                ).astype(jnp.bfloat16)
-                for a in range(2):
-                    k_s[a, rows, 0:nope] = kv[:, a * width : a * width + nope]
-                    k_s[a, rows, nope:] = kr[group, a, rows, :]
-                    v_s[a, rows, :] = kv[:, a * width + nope : (a + 1) * width]
-            for a in range(2):
-                for r in range(2):
-                    rows = pl.ds(r * tile, tile)
-                    span = (r + 1) * tile
-                    scores = lax.dot_general(
-                        q_s[a, rows, :], k_s[a, 0:span, :], (((1,), (1,)), ((), ())),
-                        preferred_element_type=jnp.float32,
-                    )
-                    scores = scores + bias[group, rows, 0:span]
-                    top = jnp.max(scores, axis=-1, keepdims=True)
-                    terms = jnp.exp2((scores - top) * factor)
-                    total = jnp.sum(terms, axis=-1, keepdims=True)
-                    mixed = jnp.dot(
-                        terms.astype(jnp.bfloat16), v_s[a, 0:span, :], preferred_element_type=jnp.float32
-                    )
-                    at = (2 * j + a) * vd
-                    obuf[group, block, rows, at : at + vd] = (mixed / total).astype(jnp.bfloat16)
-
-    def columns(block):
-        width = nh * vd
-        return pl.ds(pl.multiple_of((2 * block + parity) * width, width), width)
-
-    def local_out(block):
-        return pltpu.make_async_copy(obuf.at[0, block], out.at[:, columns(block)], out_local.at[block])
-
-    def pair_out(block):
+                scores = scores + bias[group, rows, 0:span]
+                top = jnp.max(scores, axis=-1, keepdims=True)
+                terms = jnp.exp2((scores - top) * factor)
+                total = jnp.sum(terms, axis=-1, keepdims=True)
+                mixed = jnp.dot(
+                    terms.astype(jnp.bfloat16), v_s[a, 0:span, :], preferred_element_type=jnp.float32
+                )
+                obuf[group, block, j, rows, a * vd : (a + 1) * vd] = (mixed / total).astype(jnp.bfloat16)
+
+    def columns(owner, block, j):
+        return pl.ds(pl.multiple_of(((2 * block + owner) * per + j) * 2 * vd, 2 * vd), 2 * vd)
+
+    def local_out(block, j):
+        return pltpu.make_async_copy(
+            obuf.at[0, block, j], out.at[:, columns(parity, block, j)], out_local.at[block, j]
+        )
+
+    def pair_out(block, j, owner):
         return pltpu.make_async_remote_copy(
-            src_ref=obuf.at[1, block], dst_ref=out.at[:, columns(block)],
-            send_sem=out_send.at[block], recv_sem=out_recv.at[block],
-            device_id=pair, device_id_type=MESH,
-        )
-
-    def pair_out_wait(block):
-        width = nh * vd
-        span = pl.ds(pl.multiple_of((2 * block + 1 - parity) * width, width), width)
-        return pltpu.make_async_remote_copy(
-            src_ref=obuf.at[1, block], dst_ref=out.at[:, span],
-            send_sem=out_send.at[block], recv_sem=out_recv.at[block],
+            src_ref=obuf.at[1, block, j], dst_ref=out.at[:, columns(owner, block, j)],
+            send_sem=out_send.at[block, j], recv_sem=out_recv.at[block, j],
             device_id=pair, device_id_type=MESH,
         )
 
@@ -263,60 +268,95 @@
     normalize(0, core)
     lat_copy(latents, 0, 1 - core, sibling, 0).wait_recv()
     normalize(0, 1 - core)
-    own_wq.wait()
-    own_wkv.wait()
-
-    def own_step(g, carry):
-        @pl.when(g == 1)
-        def _():
-            forward(1, 0)
+    forward(1, 0)
+
+    def own_step(u, carry):
+        g, j = u // per, lax.rem(u, per)
+
+        @pl.when(u == per)
+        def _():
+            forward(1, 2)
             lat_copy(latents, 1, core, pair, 1).wait_recv()
             lat_copy(lat.at[1, core], 1, core, sibling, 2).start()
+            forward(1, 3)
             normalize(1, core)
             lat_copy(lat.at[1, 1 - core], 1, 1 - core, sibling, 2).wait_recv()
             normalize(1, 1 - core)
+            forward(1, 4)
+
+        attend(pos, g, j)
+
+        @pl.when(u == 0)
+        def _():
             forward(1, 1)
 
-        attend(pos, g)
+        @pl.when(g == 0)
+        def _():
+            local_out(pos, j).start()
+
+        @pl.when(g == 1)
+        def _():
+            pair_out(pos, j, parity).start()
+
         return carry
 
-    lax.fori_loop(0, 2, own_step, 0)
-    local_out(pos).start()
-    pair_out(pos).start()
-    forward(1, 2)
-
-    def stage(t, carry):
-        @pl.when(t < n_line)
-        def _():
-            for chunk in range(CHUNKS):
-                forward(t, chunk)
-
-        def side(s, inner):
-            block = pos + (2 * s - 1) * (t - 1)
+    lax.fori_loop(0, 2 * per, own_step, 0)
+    forward(1, 5)
+
+    def work(t, first, count, wait):
+        def side(n, inner):
+            block = pos + (2 * n - 1) * t
 
             @pl.when((block >= 0) & (block < n_line))
             def _():
                 held = jnp.clip(block, 0, n_line - 1)
-                for chunk in range(CHUNKS):
-                    x_copy(held, chunk, 1 - half).wait_recv()
-
-                def group_step(i, rest):
-                    attend(held, 1 - i)
-
-                    @pl.when(i == 0)
+
+                @pl.when(wait)
+                def _():
+                    for chunk in range(CHUNKS):
+                        x_copy(held, chunk, 1 - half).wait_recv()
+
+                def unit_step(i, rest):
+                    j, g = first + i // 2, 1 - lax.rem(i, 2)
+                    attend(held, g, j)
+
+                    @pl.when(g == 1)
                     def _():
-                        pair_out(held).start()
+                        pair_out(held, j, parity).start()
+
+                    @pl.when(g == 0)
+                    def _():
+                        local_out(held, j).start()
 
                     return rest
 
-                lax.fori_loop(0, 2, group_step, 0)
-                local_out(held).start()
+                lax.fori_loop(0, 2 * count, unit_step, 0)
 
             return inner
 
-        return lax.fori_loop(0, 2, side, carry)
-
-    lax.fori_loop(2, n_line + 1, stage, 0)
+        lax.fori_loop(0, 2, side, 0)
+
+    def stage(i, carry):
+        t, late = i // 2, lax.rem(i, 2) == 0
+
+        @pl.when(late & (t < n_line))
+        def _():
+            for chunk in range(CHUNKS):
+                forward(t, chunk)
+
+        if split:
+            count = per // 2
+            first = jnp.where(late, 1 - half, half) * count
+            work(jnp.where(late, t - 1, t), first, count, late)
+        else:
+
+            @pl.when(late)
+            def _():
+                work(t - 1, 0, per, late)
+
+        return carry
+
+    lax.fori_loop(4 - int(split), 2 * n_line + 1, stage, 0)
 
     lat_copy(latents, 0, core, sibling, 0).wait_send()
     lat_copy(latents, 1, core, pair, 1).wait_send()
@@ -338,9 +378,10 @@
             for chunk in range(CHUNKS):
                 x_copy(block, chunk, half).wait_send()
 
-        local_out(block).wait()
-        pair_out(block).wait_send()
-        pair_out_wait(block).wait_recv()
+        for j in range(per):
+            local_out(block, j).wait()
+            pair_out(block, j, parity).wait_send()
+            pair_out(block, j, 1 - parity).wait_recv()
         return carry
 
     lax.fori_loop(0, n_line, drain, 0)
@@ -359,19 +400,8 @@
     slots = lengths.shape[1]
     r = rope // 2
 
-    body = q_width + kv_width
-    first, second = latents[:, body : body + r], latents[:, body + r :]
-    lat = jnp.concatenate([latents[:, :body], first, first, second, second], axis=1)
-    wide = lat.shape[1]
-    q4 = q_weight[0].reshape(q_width, nh // 2, 2, nope + rope)
-    wq = jnp.concatenate(
-        [
-            q4[:, :, 0, :nope], q4[:, :, 1, :nope],
-            q4[:, :, 0, nope : nope + r], q4[:, :, 1, nope : nope + r],
-            q4[:, :, 0, nope + r :], q4[:, :, 1, nope + r :],
-        ],
-        axis=-1,
-    ).reshape(q_width, nh * (nope + rope))
+    wide = latents.shape[1]
+    wq = jnp.transpose(q_weight[0], (1, 2, 0)).reshape(nh * (nope + rope), q_width)
     wkv = kv_weight[0].reshape(kv_width, nh * (nope + vd))
     base = 10000.0 ** (-2.0 * np.arange(r) / rope)
     freqs = jnp.asarray(np.tile(base, 4)[None, :], jnp.float32)
@@ -387,7 +417,7 @@
         out_specs=hbm,
         scratch_shapes=[
             pltpu.VMEM((n_line,) + wq.shape, bf16),
-            pltpu.VMEM((n_line,) + wkv.shape, bf16),
+            pltpu.VMEM((n_line, 2, kv_width, nh * (nope + vd) // 2), bf16),
             pltpu.VMEM((2, 2, half_tokens, wide), bf16),
             pltpu.VMEM((2, tokens, q_width), bf16),
             pltpu.VMEM((2, tokens, kv_width), bf16),
@@ -398,16 +428,16 @@
             pltpu.VMEM((2, tokens, nope + 128), bf16),
             pltpu.VMEM((2, tokens, nope + 128), bf16),
             pltpu.VMEM((2, tokens, vd), bf16),
-            pltpu.VMEM((2, n_line, tokens, nh * vd), bf16),
-            dma((3,)), dma((3,)), dma((3,)),
+            pltpu.VMEM((2, n_line, nh // 2, tokens, 2 * vd), bf16),
+            dma((3 * nh + 3,)), dma((3,)), dma((3,)),
             dma((2, n_line, CHUNKS)), dma((n_line, CHUNKS)),
             dma((n_line, CHUNKS)), dma((n_line, CHUNKS)),
-            dma((n_line,)), dma((n_line,)), dma((n_line,)),
+            dma((n_line, nh // 2)), dma((n_line, nh // 2)), dma((n_line, nh // 2)),
         ],
         compiler_params=pltpu.CompilerParams(
             collective_id=0, has_side_effects=True, vmem_limit_bytes=60 * 1024 * 1024
         ),
-    )(lengths, freqs, q_gain[None, :], kv_gain[None, :], lat, wq, wkv)
+    )(lengths, freqs, q_gain[None, :], kv_gain[None, :], latents, wq, wkv)
 
 
 def solution(mesh):

time: 194 us -> 149 us (0.77)
  local copies, waits for them, and re-layouts: 42.2 us -> 10 us
  Pallas kernels: 150 us -> 139 us
    concatenate x2 -> x0, local copies, waits for them, and re-layouts: 20.5 us -> none  [the longest x1 18.6 us: shards(): jnp.concatenate([q4[:, :, 0, :nope], q4[:, :, 1, :nope], q4[:, :, 0, nope...]
    pallas_call x1, Pallas kernels: 150 us -> 139 us  [shards(): pl.pallas_call(functools.partial(kernel, n_line, nh, q_width, kv_width, r...]
    unnamed x16 -> x5, local copies, waits for them, and re-layouts: 18.3 us -> 8.62 us
    slice x8 -> x0, local copies, waits for them, and re-layouts: 2.77 us -> none  [the longest x1 1.47 us: shards(): q4[:, :, 1, :nope]]
where the time goes in v2:
time: 149 us
  Pallas kernels  139 us (93%)
  local copies, waits for them, and re-layouts  10 us (7%)
    pallas_call x1, Pallas kernels, shards(): pl.pallas_call(functools.partial(kernel, n_line, nh, q_width, kv_width, r...  139 us
    unnamed x5, local copies, waits for them, and re-layouts  8.62 us

profile of v2, /device:TPU:0, one launch (start us, length us, event | category | flops | bytes accessed | tf_op | source)
XLA Modules:
  0.0 149.0 jit_solution(8915968534749545220)
XLA Ops:
  0.0 0.0 copy-start
  0.0 1.4 broadcast_in_dim.6.q_gain
  1.4 2.4 %copy.9 = bf16[64,8,4,256]{3,1,2,0:T(8,128)(2,1)} copy(bf16[64,8,4,256]{3,2,1,0:T(4,128)(2,1)} %bitcast.11) | data formatting | bytes 2097152
  3.8 0.0 copy-done
  3.8 1.5 %copy.8.latents = bf16[256,2112]{1,0:T(8,128)(2,1)} copy(bf16[256,2112]{0,1:T(8,128)(2,1)S(1)} %copy-done) | data formatting | bytes 2162688 | tf_op args[0]
  5.3 139.0 %shard_map.73 = bf16[512,4096]{1,0:T(8,128)(2,1)} custom-call(s32[8,8]{1,0:T(8,128)} %lengths.1, f32[1,128]{1,0:T(1,128)} %constant.2.clone.freqs, f32[1,1536]{1,0:T(1,128)} %broadcast_in_dim.6.q_gain, f32[1,512]{1,0:T(1,128)} %bitcast.12, bf16[256,2112]{1,0:T(8,128)(2,1)} %copy.8.latents, bf16[768,1536]{1,0:T(8,128)(2,1)} %bitcast.10, bf16[512,1024]{1,0:T(8,128)(2,1)} %bitcast.9), custom_call_target="tpu_custom_call" | custom-call | tf_op jit(solution)/shard_map/pallas_call | solution.py:413
  144.3 4.7 %copy.11 = bf16[512,4096]{1,0:T(8,128)(2,1)} copy(bf16[512,4096]{1,0:T(8,128)(2,1)} %shard_map.73) | data formatting | bytes 8388608
Async XLA Ops:
  0.0 3.8 %copy-start = (bf16[256,2112]{0,1:T(8,128)(2,1)S(1)}, bf16[256,2112]{0,1:T(8,128)(2,1)}, u32[]{:S(2)}) copy-start(bf16[256,2112]{0,1:T(8,128)(2,1)} %param.7) | copy-start | bytes 3244036

commit v3 on v2

--- a/solution.py
+++ b/solution.py
@@ -19,8 +19,8 @@
     n_line, nh, q_width, kv_width, rope, nope, vd, tokens, slots,
     lengths, freqs, q_gain, kv_gain, latents, wq, wkv,
     out,
-    wq_buf, wkv_buf, lat, qn, kvn, cosine, sine, kr, bias, q_s, k_s, v_s, obuf,
-    own_sem, lat_send, lat_recv, line_send, line_recv, x_send, x_recv, out_local, out_send, out_recv,
+    wq_buf, wkv_buf, lat, qn, kvn, cosine, sine, kr, bias, q_s, k_s, v_s, obuf, gains, turned_lat,
+    own_sem, lat_send, lat_recv, line_send, line_recv, x_send, x_recv, out_send, out_recv,
 ):
     part = lax.axis_index("parts")
     seq = lax.axis_index("seq")
@@ -50,9 +50,13 @@
             return wq_buf.at[block, pl.ds(start, q_rows), :]
         return wkv_buf.at[block, side, pl.ds((chunk - 4) * kv_rows, kv_rows), :]
 
+    def at_end(block):
+        return (block == 0) | (block == n_line - 1)
+
     def line_copy(block, chunk, direction):
+        held = slot(block, half, chunk) if chunk < CHUNKS else slot(block, 1 - half, CHUNKS - 1)
         return pltpu.make_async_remote_copy(
-            src_ref=slot(block, half, chunk), dst_ref=slot(block, half, chunk),
+            src_ref=held, dst_ref=held,
             send_sem=line_send.at[direction, block, chunk], recv_sem=line_recv.at[block, chunk],
             device_id=(left, right)[direction], device_id_type=MESH,
         )
@@ -83,7 +87,7 @@
     def _():
         pl.semaphore_signal(barrier, inc=1, device_id=right, device_id_type=MESH)
 
-    own_lat = pltpu.make_async_copy(latents, lat.at[0, core], own_sem.at[0])
+    own_lat = pltpu.make_async_copy(latents, turned_lat, own_sem.at[0])
     own = []
     for h in range(nh):
         j, a = h // 2, h % 2
@@ -100,8 +104,6 @@
 
     pl.semaphore_wait(barrier, 3 + has_left.astype(jnp.int32) + has_right.astype(jnp.int32))
 
-    lat_copy(latents, 0, core, sibling, 0).start()
-    lat_copy(latents, 1, core, pair, 1).start()
     for copy in own:
         copy.wait()
 
@@ -110,33 +112,45 @@
         for chunk in range(CHUNKS):
             line_copy(pos, chunk, 0).start()
 
+        @pl.when(at_end(pos))
+        def _():
+            line_copy(pos, CHUNKS, 0).start()
+
     @pl.when(has_right)
     def _():
         for chunk in range(CHUNKS):
             line_copy(pos, chunk, 1).start()
 
+        @pl.when(at_end(pos))
+        def _():
+            line_copy(pos, CHUNKS, 1).start()
+
+    def pass_on(block, chunk, direction):
+        line_copy(block, chunk, 1 - direction).wait_recv()
+
+        @pl.when((has_left, has_right)[direction])
+        def _():
+            line_copy(block, chunk, direction).start()
+
+        if chunk < CHUNKS - 1:
+            x_copy(block, chunk, half).start()
+        elif chunk == CHUNKS - 1:
+
+            @pl.when(jnp.logical_not(at_end(block)))
+            def _():
+                x_copy(block, chunk, half).start()
+
     def forward(distance, chunk):
-        @pl.when(pos - distance >= 0)
-        def _():
-            block = jnp.maximum(pos - distance, 0)
-            line_copy(block, chunk, 1).wait_recv()
-
-            @pl.when(has_right)
-            def _():
-                line_copy(block, chunk, 1).start()
-
-            x_copy(block, chunk, half).start()
-
-        @pl.when(pos + distance < n_line)
-        def _():
-            block = jnp.minimum(pos + distance, n_line - 1)
-            line_copy(block, chunk, 0).wait_recv()
-
-            @pl.when(has_left)
-            def _():
-                line_copy(block, chunk, 0).start()
-
-            x_copy(block, chunk, half).start()
+        def both(condition, block, direction):
+            if chunk == CHUNKS:
+                condition = condition & at_end(block)
+
+            @pl.when(condition)
+            def _():
+                pass_on(block, chunk, direction)
+
+        both(pos - distance >= 0, jnp.maximum(pos - distance, 0), 1)
+        both(pos + distance < n_line, jnp.minimum(pos + distance, n_line - 1), 0)
 
     unit = tokens // slots
 
@@ -182,10 +196,10 @@
             target = pl.ds(pl.multiple_of(owner * half_tokens + i * step_rows, step_rows), step_rows)
             q_part = lat[group, owner, source, 0:q_width].astype(jnp.float32)
             squares = jnp.mean(q_part * q_part, axis=-1, keepdims=True)
-            qn[group, target, :] = (q_part * lax.rsqrt(squares + EPSILON) * q_gain[...]).astype(jnp.bfloat16)
+            qn[group, target, :] = (q_part * lax.rsqrt(squares + EPSILON) * gains[0:1, 0:q_width]).astype(jnp.bfloat16)
             kv_part = lat[group, owner, source, q_width : q_width + kv_width].astype(jnp.float32)
             squares = jnp.mean(kv_part * kv_part, axis=-1, keepdims=True)
-            kvn[group, target, :] = (kv_part * lax.rsqrt(squares + EPSILON) * kv_gain[...]).astype(jnp.bfloat16)
+            kvn[group, target, :] = (kv_part * lax.rsqrt(squares + EPSILON) * gains[0:1, q_width : q_width + kv_width]).astype(jnp.bfloat16)
             tail = lat[group, owner, source, q_width + kv_width :].astype(jnp.float32)
             tail = jnp.concatenate([tail, tail], axis=1)
             lanes = lax.broadcasted_iota(jnp.int32, tail.shape, 1)
@@ -246,27 +260,39 @@
                 mixed = jnp.dot(
                     terms.astype(jnp.bfloat16), v_s[a, 0:span, :], preferred_element_type=jnp.float32
                 )
-                obuf[group, block, j, rows, a * vd : (a + 1) * vd] = (mixed / total).astype(jnp.bfloat16)
+                mixed = (mixed / total).astype(jnp.bfloat16)
+                at = pl.multiple_of(((2 * block + parity) * per + j) * 2 * vd + a * vd, vd)
+
+                @pl.when(group == 0)
+                def _():
+                    out[rows, pl.ds(at, vd)] = mixed
+
+                @pl.when(group == 1)
+                def _():
+                    obuf[block, j, rows, a * vd : (a + 1) * vd] = mixed
 
     def columns(owner, block, j):
         return pl.ds(pl.multiple_of(((2 * block + owner) * per + j) * 2 * vd, 2 * vd), 2 * vd)
 
-    def local_out(block, j):
-        return pltpu.make_async_copy(
-            obuf.at[0, block, j], out.at[:, columns(parity, block, j)], out_local.at[block, j]
-        )
-
     def pair_out(block, j, owner):
         return pltpu.make_async_remote_copy(
-            src_ref=obuf.at[1, block, j], dst_ref=out.at[:, columns(owner, block, j)],
+            src_ref=obuf.at[block, j], dst_ref=out.at[:, columns(owner, block, j)],
             send_sem=out_send.at[block, j], recv_sem=out_recv.at[block, j],
             device_id=pair, device_id_type=MESH,
         )
 
+    own_lat.wait()
+    wide = turned_lat.shape[0]
+    for low in range(0, wide, 128):
+        high = min(low + 128, wide)
+        lat[0, core, :, low:high] = turned_lat[low:high, :].T
+    gains[0:1, 0:q_width] = q_gain[...].reshape(1, q_width)
+    gains[0:1, q_width:] = kv_gain[...].reshape(1, kv_width)
     lax.fori_loop(0, 2, lambda g, c: (tables(g), c)[1], 0)
-    own_lat.wait()
+    lat_copy(lat.at[0, core], 0, core, sibling, 0).start()
+    lat_copy(lat.at[0, core], 1, core, pair, 1).start()
     normalize(0, core)
-    lat_copy(latents, 0, 1 - core, sibling, 0).wait_recv()
+    lat_copy(lat.at[0, core], 0, 1 - core, sibling, 0).wait_recv()
     normalize(0, 1 - core)
     forward(1, 0)
 
@@ -276,7 +302,7 @@
         @pl.when(u == per)
         def _():
             forward(1, 2)
-            lat_copy(latents, 1, core, pair, 1).wait_recv()
+            lat_copy(lat.at[0, core], 1, core, pair, 1).wait_recv()
             lat_copy(lat.at[1, core], 1, core, sibling, 2).start()
             forward(1, 3)
             normalize(1, core)
@@ -290,10 +316,6 @@
         def _():
             forward(1, 1)
 
-        @pl.when(g == 0)
-        def _():
-            local_out(pos, j).start()
-
         @pl.when(g == 1)
         def _():
             pair_out(pos, j, parity).start()
@@ -302,6 +324,7 @@
 
     lax.fori_loop(0, 2 * per, own_step, 0)
     forward(1, 5)
+    forward(1, CHUNKS)
 
     def work(t, first, count, wait):
         def side(n, inner):
@@ -313,8 +336,12 @@
 
                 @pl.when(wait)
                 def _():
-                    for chunk in range(CHUNKS):
+                    for chunk in range(CHUNKS - 1):
                         x_copy(held, chunk, 1 - half).wait_recv()
+
+                    @pl.when(jnp.logical_not(at_end(held)))
+                    def _():
+                        x_copy(held, CHUNKS - 1, 1 - half).wait_recv()
 
                 def unit_step(i, rest):
                     j, g = first + i // 2, 1 - lax.rem(i, 2)
@@ -324,10 +351,6 @@
                     def _():
                         pair_out(held, j, parity).start()
 
-                    @pl.when(g == 0)
-                    def _():
-                        local_out(held, j).start()
-
                     return rest
 
                 lax.fori_loop(0, 2 * count, unit_step, 0)
@@ -341,7 +364,7 @@
 
         @pl.when(late & (t < n_line))
         def _():
-            for chunk in range(CHUNKS):
+            for chunk in range(CHUNKS + 1):
                 forward(t, chunk)
 
         if split:
@@ -358,28 +381,32 @@
 
     lax.fori_loop(4 - int(split), 2 * n_line + 1, stage, 0)
 
-    lat_copy(latents, 0, core, sibling, 0).wait_send()
-    lat_copy(latents, 1, core, pair, 1).wait_send()
+    lat_copy(lat.at[0, core], 0, core, sibling, 0).wait_send()
+    lat_copy(lat.at[0, core], 1, core, pair, 1).wait_send()
     lat_copy(lat.at[1, core], 1, core, sibling, 2).wait_send()
 
     def drain(block, carry):
-        @pl.when((block <= pos) & has_right)
-        def _():
-            for chunk in range(CHUNKS):
-                line_copy(block, chunk, 1).wait_send()
-
-        @pl.when((block >= pos) & has_left)
-        def _():
-            for chunk in range(CHUNKS):
-                line_copy(block, chunk, 0).wait_send()
+        for goes, direction in (((block <= pos) & has_right, 1), ((block >= pos) & has_left, 0)):
+
+            @pl.when(goes)
+            def _():
+                for chunk in range(CHUNKS):
+                    line_copy(block, chunk, direction).wait_send()
+
+                @pl.when(at_end(block))
+                def _():
+                    line_copy(block, CHUNKS, direction).wait_send()
 
         @pl.when(block != pos)
         def _():
-            for chunk in range(CHUNKS):
+            for chunk in range(CHUNKS - 1):
                 x_copy(block, chunk, half).wait_send()
 
+            @pl.when(jnp.logical_not(at_end(block)))
+            def _():
+                x_copy(block, CHUNKS - 1, half).wait_send()
+
         for j in range(per):
-            local_out(block, j).wait()
             pair_out(block, j, parity).wait_send()
             pair_out(block, j, 1 - parity).wait_recv()
         return carry
@@ -412,9 +439,9 @@
     heads_total = nh * n_seq
     return pl.pallas_call(
         functools.partial(kernel, n_line, nh, q_width, kv_width, rope, nope, vd, tokens, slots),
-        out_shape=jax.ShapeDtypeStruct((tokens, heads_total * vd), bf16),
+        out_shape=pltpu.VMEM((tokens, heads_total * vd), bf16),
         in_specs=[pl.BlockSpec(memory_space=pltpu.SMEM), vmem, vmem, vmem, hbm, hbm, hbm],
-        out_specs=hbm,
+        out_specs=vmem,
         scratch_shapes=[
             pltpu.VMEM((n_line,) + wq.shape, bf16),
             pltpu.VMEM((n_line, 2, kv_width, nh * (nope + vd) // 2), bf16),
@@ -428,16 +455,18 @@
             pltpu.VMEM((2, tokens, nope + 128), bf16),
             pltpu.VMEM((2, tokens, nope + 128), bf16),
             pltpu.VMEM((2, tokens, vd), bf16),
-            pltpu.VMEM((2, n_line, nh // 2, tokens, 2 * vd), bf16),
+            pltpu.VMEM((n_line, nh // 2, tokens, 2 * vd), bf16),
+            pltpu.VMEM((8, q_width + kv_width), f32),
+            pltpu.VMEM((wide, half_tokens), bf16),
             dma((3 * nh + 3,)), dma((3,)), dma((3,)),
-            dma((2, n_line, CHUNKS)), dma((n_line, CHUNKS)),
+            dma((2, n_line, CHUNKS + 1)), dma((n_line, CHUNKS + 1)),
             dma((n_line, CHUNKS)), dma((n_line, CHUNKS)),
-            dma((n_line, nh // 2)), dma((n_line, nh // 2)), dma((n_line, nh // 2)),
+            dma((n_line, nh // 2)), dma((n_line, nh // 2)),
         ],
         compiler_params=pltpu.CompilerParams(
-            collective_id=0, has_side_effects=True, vmem_limit_bytes=60 * 1024 * 1024
+            collective_id=0, has_side_effects=True, vmem_limit_bytes=59 * 1024 * 1024
         ),
-    )(lengths, freqs, q_gain[None, :], kv_gain[None, :], latents, wq, wkv)
+    )(lengths, freqs, q_gain, kv_gain, latents.T, wq, wkv)
 
 
 def solution(mesh):

time: 149 us -> 151 us (1.013)
  Pallas kernels: 139 us -> 146 us
  local copies, waits for them, and re-layouts: 10 us -> 4.44 us
    pallas_call x1, Pallas kernels: 139 us -> 146 us  [shards(): pl.pallas_call(functools.partial(kernel, n_line, nh, q_width, kv_width, r...]
    unnamed x5 -> x2, local copies, waits for them, and re-layouts: 8.62 us -> 4.44 us
where the time goes in v3:
time: 151 us; the launch traced here: 150 us
  Pallas kernels  146 us (97%)
  local copies, waits for them, and re-layouts  4.44 us (3%)
    pallas_call x1, Pallas kernels, shards(): pl.pallas_call(functools.partial(kernel, n_line, nh, q_width, kv_width, r...  146 us
    unnamed x2, local copies, waits for them, and re-layouts  4.44 us

profile of v3, /device:TPU:0, one launch (start us, length us, event | category | flops | bytes accessed | tf_op | source)
XLA Modules:
  0.0 150.4 jit_solution(16786747977991898461)
XLA Ops:
  0.0 2.4 %copy.8 = bf16[64,8,4,256]{3,1,2,0:T(8,128)(2,1)} copy(bf16[64,8,4,256]{3,2,1,0:T(4,128)(2,1)} %bitcast.12) | data formatting | bytes 2097152
  2.4 146.0 %shard_map.73 = bf16[512,4096]{1,0:T(8,128)(2,1)S(1)} custom-call(s32[8,8]{1,0:T(8,128)} %lengths.1, f32[1,128]{1,0:T(1,128)} %constant.2.clone.freqs, f32[1536]{0:T(1024)} %q_gain.1, f32[512]{0:T(512)} %kv_gain.1, bf16[2112,256]{1,0:T(8,128)(2,1)} %bitcast.11, bf16[768,1536]{1,0:T(8,128)(2,1)} %bitcast.10, bf16[512,1024]{1,0:T(8,128)(2,1)} %bitcast.9), custom_call_target="tpu_custom_call" | custom-call | tf_op jit(solution)/shard_map/pallas_call | solution.py:440
  148.4 2.0 %copy.10 = bf16[512,4096]{1,0:T(8,128)(2,1)} copy(bf16[512,4096]{1,0:T(8,128)(2,1)S(1)} %shard_map.73) | data formatting | bytes 8388608

commit v4 on v3

--- a/solution.py
+++ b/solution.py
@@ -12,6 +12,7 @@
 EPSILON = 1e-06
 MASKED = -1e30
 CHUNKS = 6
+EXTRA = 3
 MESH = pl.DeviceIdType.MESH
 
 
@@ -53,8 +54,11 @@
     def at_end(block):
         return (block == 0) | (block == n_line - 1)
 
+    def direct(block):
+        return at_end(block) & (jnp.abs(pos - block) == 1)
+
     def line_copy(block, chunk, direction):
-        held = slot(block, half, chunk) if chunk < CHUNKS else slot(block, 1 - half, CHUNKS - 1)
+        held = slot(block, half, chunk) if chunk < CHUNKS else slot(block, 1 - half, chunk - EXTRA)
         return pltpu.make_async_remote_copy(
             src_ref=held, dst_ref=held,
             send_sem=line_send.at[direction, block, chunk], recv_sem=line_recv.at[block, chunk],
@@ -114,7 +118,8 @@
 
         @pl.when(at_end(pos))
         def _():
-            line_copy(pos, CHUNKS, 0).start()
+            for chunk in range(CHUNKS, CHUNKS + EXTRA):
+                line_copy(pos, chunk, 0).start()
 
     @pl.when(has_right)
     def _():
@@ -123,7 +128,8 @@
 
         @pl.when(at_end(pos))
         def _():
-            line_copy(pos, CHUNKS, 1).start()
+            for chunk in range(CHUNKS, CHUNKS + EXTRA):
+                line_copy(pos, chunk, 1).start()
 
     def pass_on(block, chunk, direction):
         line_copy(block, chunk, 1 - direction).wait_recv()
@@ -132,19 +138,16 @@
         def _():
             line_copy(block, chunk, direction).start()
 
-        if chunk < CHUNKS - 1:
+        if chunk < CHUNKS - EXTRA:
             x_copy(block, chunk, half).start()
-        elif chunk == CHUNKS - 1:
-
-            @pl.when(jnp.logical_not(at_end(block)))
+        else:
+
+            @pl.when(jnp.logical_not(direct(block)))
             def _():
                 x_copy(block, chunk, half).start()
 
     def forward(distance, chunk):
         def both(condition, block, direction):
-            if chunk == CHUNKS:
-                condition = condition & at_end(block)
-
             @pl.when(condition)
             def _():
                 pass_on(block, chunk, direction)
@@ -324,7 +327,6 @@
 
     lax.fori_loop(0, 2 * per, own_step, 0)
     forward(1, 5)
-    forward(1, CHUNKS)
 
     def work(t, first, count, wait):
         def side(n, inner):
@@ -336,12 +338,18 @@
 
                 @pl.when(wait)
                 def _():
-                    for chunk in range(CHUNKS - 1):
+                    for chunk in range(CHUNKS - EXTRA):
                         x_copy(held, chunk, 1 - half).wait_recv()
 
-                    @pl.when(jnp.logical_not(at_end(held)))
+                    @pl.when(direct(held))
                     def _():
-                        x_copy(held, CHUNKS - 1, 1 - half).wait_recv()
+                        for chunk in range(CHUNKS, CHUNKS + EXTRA):
+                            line_copy(held, chunk, 0).wait_recv()
+
+                    @pl.when(jnp.logical_not(direct(held)))
+                    def _():
+                        for chunk in range(CHUNKS - EXTRA, CHUNKS):
+                            x_copy(held, chunk, 1 - half).wait_recv()
 
                 def unit_step(i, rest):
                     j, g = first + i // 2, 1 - lax.rem(i, 2)
@@ -364,8 +372,18 @@
 
         @pl.when(late & (t < n_line))
         def _():
-            for chunk in range(CHUNKS + 1):
+            for chunk in range(CHUNKS // 2):
                 forward(t, chunk)
+
+        outer = jnp.logical_not(has_left & has_right)
+
+        def rest_of(t):
+            for chunk in range(CHUNKS // 2, CHUNKS):
+                forward(t, chunk)
+
+        @pl.when(late & (t < n_line) & jnp.logical_not(outer))
+        def _():
+            rest_of(t)
 
         if split:
             count = per // 2
@@ -377,6 +395,10 @@
             def _():
                 work(t - 1, 0, per, late)
 
+        @pl.when(late & (t < n_line) & outer)
+        def _():
+            rest_of(t)
+
         return carry
 
     lax.fori_loop(4 - int(split), 2 * n_line + 1, stage, 0)
@@ -393,18 +415,20 @@
                 for chunk in range(CHUNKS):
                     line_copy(block, chunk, direction).wait_send()
 
-                @pl.when(at_end(block))
+                @pl.when(at_end(block) & (block == pos))
                 def _():
-                    line_copy(block, CHUNKS, direction).wait_send()
+                    for chunk in range(CHUNKS, CHUNKS + EXTRA):
+                        line_copy(block, chunk, direction).wait_send()
 
         @pl.when(block != pos)
         def _():
-            for chunk in range(CHUNKS - 1):
+            for chunk in range(CHUNKS - EXTRA):
                 x_copy(block, chunk, half).wait_send()
 
-            @pl.when(jnp.logical_not(at_end(block)))
+            @pl.when(jnp.logical_not(direct(block)))
             def _():
-                x_copy(block, CHUNKS - 1, half).wait_send()
+                for chunk in range(CHUNKS - EXTRA, CHUNKS):
+                    x_copy(block, chunk, half).wait_send()
 
         for j in range(per):
             pair_out(block, j, parity).wait_send()
@@ -459,7 +483,7 @@
             pltpu.VMEM((8, q_width + kv_width), f32),
             pltpu.VMEM((wide, half_tokens), bf16),
             dma((3 * nh + 3,)), dma((3,)), dma((3,)),
-            dma((2, n_line, CHUNKS + 1)), dma((n_line, CHUNKS + 1)),
+            dma((2, n_line, CHUNKS + EXTRA)), dma((n_line, CHUNKS + EXTRA)),
             dma((n_line, CHUNKS)), dma((n_line, CHUNKS)),
             dma((n_line, nh // 2)), dma((n_line, nh // 2)),
         ],

time: 151 us -> 141 us (0.934)
  Pallas kernels: 146 us -> 136 us
    pallas_call x1, Pallas kernels: 146 us -> 136 us  [shards(): pl.pallas_call(functools.partial(kernel, n_line, nh, q_width, kv_width, r...]
where the time goes in v4:
time: 141 us
  Pallas kernels  136 us (96%)
  local copies, waits for them, and re-layouts  4.44 us (3%)
    pallas_call x1, Pallas kernels, shards(): pl.pallas_call(functools.partial(kernel, n_line, nh, q_width, kv_width, r...  136 us
    unnamed x2, local copies, waits for them, and re-layouts  4.44 us

profile of v4, /device:TPU:0, one launch (start us, length us, event | category | flops | bytes accessed | tf_op | source)
XLA Modules:
  0.0 140.9 jit_solution(13272718703883724942)
XLA Ops:
  0.0 2.4 %copy.8 = bf16[64,8,4,256]{3,1,2,0:T(8,128)(2,1)} copy(bf16[64,8,4,256]{3,2,1,0:T(4,128)(2,1)} %bitcast.12) | data formatting | bytes 2097152
  2.4 136.5 %shard_map.73 = bf16[512,4096]{1,0:T(8,128)(2,1)S(1)} custom-call(s32[8,8]{1,0:T(8,128)} %lengths.1, f32[1,128]{1,0:T(1,128)} %constant.2.clone.freqs, f32[1536]{0:T(1024)} %q_gain.1, f32[512]{0:T(512)} %kv_gain.1, bf16[2112,256]{1,0:T(8,128)(2,1)} %bitcast.11, bf16[768,1536]{1,0:T(8,128)(2,1)} %bitcast.10, bf16[512,1024]{1,0:T(8,128)(2,1)} %bitcast.9), custom_call_target="tpu_custom_call" | custom-call | tf_op jit(solution)/shard_map/pallas_call | solution.py:464
  138.9 2.0 %copy.10 = bf16[512,4096]{1,0:T(8,128)(2,1)} copy(bf16[512,4096]{1,0:T(8,128)(2,1)S(1)} %shard_map.73) | data formatting | bytes 8388608

commit v5 on v4

--- a/solution.py
+++ b/solution.py
@@ -11,8 +11,8 @@
 
 EPSILON = 1e-06
 MASKED = -1e30
-CHUNKS = 6
-EXTRA = 3
+CHUNKS = 8
+EXTRA = 4
 MESH = pl.DeviceIdType.MESH
 
 
@@ -43,13 +43,13 @@
     width = nope + vd
     r = rope // 2
     q_rows = nh * head // 8
-    kv_rows = kv_width // 2
+    kv_rows = kv_width // 4
 
     def slot(block, side, chunk):
-        if chunk < 4:
-            start = pl.multiple_of(side * (4 * q_rows) + chunk * q_rows, q_rows)
+        if 2 <= chunk < 6:
+            start = pl.multiple_of(side * (4 * q_rows) + (chunk - 2) * q_rows, q_rows)
             return wq_buf.at[block, pl.ds(start, q_rows), :]
-        return wkv_buf.at[block, side, pl.ds((chunk - 4) * kv_rows, kv_rows), :]
+        return wkv_buf.at[block, side, pl.ds((chunk if chunk < 2 else chunk - 4) * kv_rows, kv_rows), :]
 
     def at_end(block):
         return (block == 0) | (block == n_line - 1)
@@ -294,30 +294,31 @@
     lax.fori_loop(0, 2, lambda g, c: (tables(g), c)[1], 0)
     lat_copy(lat.at[0, core], 0, core, sibling, 0).start()
     lat_copy(lat.at[0, core], 1, core, pair, 1).start()
+    forward(1, 0)
     normalize(0, core)
+    forward(1, 1)
     lat_copy(lat.at[0, core], 0, 1 - core, sibling, 0).wait_recv()
     normalize(0, 1 - core)
-    forward(1, 0)
 
     def own_step(u, carry):
         g, j = u // per, lax.rem(u, per)
 
         @pl.when(u == per)
         def _():
-            forward(1, 2)
+            forward(1, 3)
             lat_copy(lat.at[0, core], 1, core, pair, 1).wait_recv()
             lat_copy(lat.at[1, core], 1, core, sibling, 2).start()
-            forward(1, 3)
+            forward(1, 4)
             normalize(1, core)
             lat_copy(lat.at[1, 1 - core], 1, 1 - core, sibling, 2).wait_recv()
             normalize(1, 1 - core)
-            forward(1, 4)
+            forward(1, 5)
 
         attend(pos, g, j)
 
         @pl.when(u == 0)
         def _():
-            forward(1, 1)
+            forward(1, 2)
 
         @pl.when(g == 1)
         def _():
@@ -326,7 +327,8 @@
         return carry
 
     lax.fori_loop(0, 2 * per, own_step, 0)
-    forward(1, 5)
+    forward(1, 6)
+    forward(1, 7)
 
     def work(t, first, count, wait):
         def side(n, inner):

time: 141 us -> 141 us (level)
  no operation moved by 1% of the time
where the time goes in v5:
time: 141 us
  Pallas kernels  136 us (96%)
  local copies, waits for them, and re-layouts  4.44 us (3%)
    pallas_call x1, Pallas kernels, shards(): pl.pallas_call(functools.partial(kernel, n_line, nh, q_width, kv_width, r...  136 us
    unnamed x2, local copies, waits for them, and re-layouts  4.44 us

profile of v5, /device:TPU:0, one launch (start us, length us, event | category | flops | bytes accessed | tf_op | source)
XLA Modules:
  0.0 140.7 jit_solution(228206486061881348)
XLA Ops:
  0.0 2.4 %copy.8 = bf16[64,8,4,256]{3,1,2,0:T(8,128)(2,1)} copy(bf16[64,8,4,256]{3,2,1,0:T(4,128)(2,1)} %bitcast.12) | data formatting | bytes 2097152
  2.4 136.3 %shard_map.73 = bf16[512,4096]{1,0:T(8,128)(2,1)S(1)} custom-call(s32[8,8]{1,0:T(8,128)} %lengths.1, f32[1,128]{1,0:T(1,128)} %constant.2.clone.freqs, f32[1536]{0:T(1024)} %q_gain.1, f32[512]{0:T(512)} %kv_gain.1, bf16[2112,256]{1,0:T(8,128)(2,1)} %bitcast.11, bf16[768,1536]{1,0:T(8,128)(2,1)} %bitcast.10, bf16[512,1024]{1,0:T(8,128)(2,1)} %bitcast.9), custom_call_target="tpu_custom_call" | custom-call | tf_op jit(solution)/shard_map/pallas_call | solution.py:466
  138.7 2.0 %copy.10 = bf16[512,4096]{1,0:T(8,128)(2,1)} copy(bf16[512,4096]{1,0:T(8,128)(2,1)S(1)} %shard_map.73) | data formatting | bytes 8388608
